TPU v7x, 32 devices: a whole 2x2x4 slice. The times are simulated.
32 devices in a mesh: dp: 4 (over x, core), tensor: 4 (over z), proj: 2 (over y).
Axes of the slice: x: 2, y: 2, z: 4, core: 2. Of those that a mesh axis runs over, the one named last changes fastest.
Arguments:
- acts: bfloat16 [40, 1024, 4096], P(('dp', 'proj'), None, 'tensor'), may hold values from -6 to 6
- cotangent: bfloat16 [40, 1024, 4096], P(('dp', 'proj'), None, 'tensor'), may hold values from -6 to 6
- adapter_down: bfloat16 [4096, 128], P('tensor'), may hold values from -0.09375 to 0.09375
- adapter_up: bfloat16 [128, 4096], P(None, 'tensor'), may hold values from -0.09375 to 0.09375
- lengths: int32 [40], P(('dp', 'proj')), may hold values from 256 to 1024, as said below
- projection_rows: int32 [4, 8, 64], P('tensor', ('dp', 'proj')), may hold values from 0 to 127
- projection_blocks: bfloat16 [4, 8, 64, 256, 128], P('tensor', ('dp', 'proj')), may hold values from -2 to 2
Outputs:
- features: float32 [40, 8192], P(('dp', 'proj'), 'tensor')
Inputs may be any that keep to these rules, and one draw needn't show every extreme that they name: `lengths`: every sequence has at least 256 tokens; some sequence has exactly 1024.
All inputs are finite; a program needn't handle non-finite values.
Results may differ from a plain program's by a relative error of at most 0.0041.
Values may be sent and summed in bfloat16 or wider, within the bound.
No kernel may reach another device: no remote copies, remote signals or barrier semaphores. Data moves between devices by JAX's collectives and lax.ppermute only.
A program may use at most 128 MiB of HBM per device.

v0:
```python
import jax
import jax.numpy as jnp
from jax import lax
from jax.sharding import PartitionSpec as P


def local(acts, cotangent, adapter_down, adapter_up, lengths, projection_rows, projection_blocks):
    sequence_per_device, length, rows_of_width = acts.shape
    adapter_rank = adapter_down.shape[1]
    reduced_hidden = jnp.einsum(
        "spu,un->spn", acts, adapter_down, preferred_element_type=jnp.float32
    )
    reduced_upstream = jnp.einsum(
        "iuq,xq->iux", cotangent, adapter_up, preferred_element_type=jnp.float32
    )
    positions = jnp.arange(length, dtype=jnp.int32)
    token_weight = (positions[None, :] < lengths[:, None]).astype(jnp.float32) / lengths[
        :, None
    ].astype(jnp.float32)
    tensor_parts = lax.axis_size("tensor")
    share_len = length // tensor_parts
    h_share, u_share = (
        lax.psum_scatter(reduced_hidden, "tensor", scatter_dimension=1, tiled=True),
        lax.psum_scatter(reduced_upstream, "tensor", scatter_dimension=1, tiled=True),
    )
    first_pos = lax.axis_index("tensor") * share_len
    local_weight = lax.dynamic_slice_in_dim(token_weight, first_pos, share_len, 1)
    hidden_share = (h_share * local_weight[:, :, None]).astype(jnp.bfloat16)
    upper_share = (u_share * local_weight[:, :, None]).astype(jnp.bfloat16)
    hidden_w, upper_w = (
        lax.all_gather(hidden_share, "tensor", axis=1, tiled=True),
        lax.all_gather(upper_share, "tensor", axis=1, tiled=True),
    )
    grad_a = jnp.einsum("etd,etr->edr", acts, upper_w, preferred_element_type=jnp.float32)
    grad_b = jnp.einsum("etd,etr->edr", cotangent, hidden_w, preferred_element_type=jnp.float32)
    gradient_list = jnp.concatenate([grad_a, grad_b], axis=2).astype(jnp.bfloat16)
    rows_per_range = rows_of_width // (lax.axis_size("dp") * lax.axis_size("proj"))
    direct_gradient = gradient_list.reshape(1, sequence_per_device, rows_of_width, 2 * adapter_rank)
    landed_blocks = lax.all_to_all(
        direct_gradient, ("dp", "proj"), split_axis=2, concat_axis=0, tiled=True
    )
    incoming_blocks = landed_blocks.reshape(-1, rows_per_range, 2 * adapter_rank)
    output_block_count = projection_blocks.shape[2]
    output_block = projection_blocks.shape[4]
    row_pick = projection_rows.reshape(output_block_count)
    block_list = projection_blocks.reshape(output_block_count, 2 * adapter_rank, output_block)
    chosen = jnp.take(incoming_blocks, row_pick, axis=1)
    contrib = jnp.einsum("eok,okc->eoc", chosen, block_list, preferred_element_type=jnp.float32)
    own_rows = lax.psum_scatter(
        contrib.reshape(incoming_blocks.shape[0], output_block_count * output_block),
        ("dp", "proj"),
        scatter_dimension=0,
        tiled=True,
    )
    result = lax.psum_scatter(own_rows, "tensor", scatter_dimension=1, tiled=True)
    return result


def solution(mesh):
    placed = (
        P(("dp", "proj"), None, "tensor"),
        P(("dp", "proj"), None, "tensor"),
        P("tensor", None),
        P(None, "tensor"),
        P(("dp", "proj")),
        P("tensor", ("dp", "proj"), None),
        P("tensor", ("dp", "proj"), None, None, None),
    )
    return jax.shard_map(
        local, mesh=mesh, in_specs=placed, out_specs=P(("dp", "proj"), "tensor"), check_vma=False
    )
```

profile of v0, /device:TPU:0, one launch (start us, length us, event | category | flops | bytes accessed | tf_op | source)
XLA Modules:
  0.0 352.2 jit_solution(9748302976001722897)
XLA Ops:
  6.5 0.0 copy-start
  6.5 0.0 reduce-scatter.4.cloned.1.call-start
  6.5 0.9 copy-done
  7.5 8.4 %fusion.13 = f32[5,1024,128]{2,1,0:T(8,128)} fusion(bf16[5,1024,1024]{2,1,0:T(8,128)(2,1)} %param.8, bf16[128,1024]{1,0:T(8,128)(2,1)S(1)} %copy-done), kind=kOutput, calls=%fused_computation.18 | convolution fusion | flops 1342177280 | bytes 13369344 | tf_op jit(solution)/shard_map/iuq,xq->iux/dot_general | solution.py:13
  15.9 0.0 copy-start.2
  15.9 0.0 reduce-scatter.4.cloned.1.call-update
  15.9 0.0 reduce-scatter.6.cloned.1.call-start
  15.9 0.9 copy-done.2
  16.8 8.4 %fusion.11 = f32[5,1024,128]{2,1,0:T(8,128)} fusion(bf16[5,1024,1024]{2,1,0:T(8,128)(2,1)} %param.7, bf16[1024,128]{1,0:T(8,128)(2,1)S(1)} %copy-done.2), kind=kOutput, calls=%fused_computation.16 | convolution fusion | flops 1342177280 | bytes 13369344 | tf_op jit(solution)/shard_map/spu,un->spn/dot_general | solution.py:10
  25.2 0.0 copy-start.3
  25.2 0.0 reduce-scatter.6.cloned.1.call-update
  25.2 0.0 all-gather.3.cloned.1.call-start
  25.3 0.6 copy-done.3
  25.9 0.1 convert_divide_fusion
  25.9 45.1 %reduce-scatter.4.cloned.1.call-done = f32[5,256,128]{2,1,0:T(8,128)} async-done(((f32[5,1024,128]{2,1,0:T(8,128)}), f32[5,256,128]{2,1,0:T(8,128)}) %reduce-scatter.4.cloned.1.call-update) | async-done | bytes 655376 | tf_op jit(solution)/shard_map/reduce_scatter | solution.py:24
  71.0 54.1 %reduce-scatter.6.cloned.1.call-done = f32[5,256,128]{2,1,0:T(8,128)} async-done(((f32[5,1024,128]{2,1,0:T(8,128)}), f32[5,256,128]{2,1,0:T(8,128)}) %reduce-scatter.6.cloned.1.call-update) | async-done | bytes 655376 | tf_op jit(solution)/shard_map/reduce_scatter | solution.py:23
  125.2 2.4 multiply_convert_fusion.1
  127.5 0.0 all-gather.3.cloned.1.call-update
  127.6 0.0 all-gather.5.cloned.1.call-start
  127.6 0.5 all-gather.5.cloned.1.call-update
  128.1 31.6 %all-gather.3.cloned.1.call-done = bf16[5,1024,128]{2,1,0:T(8,128)(2,1)} async-done(((bf16[5,256,128]{2,1,0:T(8,128)(2,1)}), bf16[5,1024,128]{2,1,0:T(8,128)(2,1)}) %all-gather.3.cloned.1.call-update) | async-done | bytes 1310736 | tf_op jit(solution)/shard_map/all_gather | solution.py:32
  159.8 7.1 %fusion.5 = bf16[1,5,1024,128]{2,3,1,0:T(8,128)(2,1)} fusion(bf16[5,1024,128]{2,1,0:T(8,128)(2,1)} %all-gather.3.cloned.1.call-done, bf16[5,1024,1024]{2,1,0:T(8,128)(2,1)} %param.7), kind=kOutput, calls=%fused_computation.7 | convolution fusion | flops 1342832640 | bytes 13107200 | tf_op jit(solution)/shard_map/etd,etr->edr/dot_general | solution.py:34
  166.9 26.0 %all-gather.5.cloned.1.call-done = bf16[5,1024,128]{2,1,0:T(8,128)(2,1)} async-done(((bf16[5,256,128]{2,1,0:T(8,128)(2,1)}), bf16[5,1024,128]{2,1,0:T(8,128)(2,1)}) %all-gather.5.cloned.1.call-update) | async-done | bytes 1310736 | tf_op jit(solution)/shard_map/all_gather | solution.py:31
  192.9 0.0 copy-start.1
  192.9 6.1 %fusion.6 = bf16[1,5,1024,128]{2,3,1,0:T(8,128)(2,1)S(1)} fusion(bf16[5,1024,128]{2,1,0:T(8,128)(2,1)} %all-gather.5.cloned.1.call-done, bf16[5,1024,1024]{2,1,0:T(8,128)(2,1)} %param.8), kind=kOutput, calls=%fused_computation.8 | convolution fusion | flops 1342832640 | bytes 13107200 | tf_op jit(solution)/shard_map/etd,etr->edr/dot_general | solution.py:35
  199.0 0.0 copy-done.1
  199.0 0.2 pad_maximum_fusion
  199.2 4.9 %copy.18 = bf16[1,5,1024,256]{3,1,0,2:T(8,128)(2,1)} copy(bf16[1,5,1024,256]{2,3,1,0:T(8,128)(2,1)S(1)} %pad_maximum_fusion) | data formatting | bytes 5242880 | tf_op jit(solution)/shard_map/concatenate | solution.py:36
  204.1 0.0 copy-start.4
  204.1 4.7 %all-to-all-start = ((bf16[1,5,1024,256]{3,1,0,2:T(8,128)(2,1)}), bf16[1,5,1024,256]{3,1,0,2:T(8,128)(2,1)}, u32[]{:S(2)}, u32[]{:S(2)}) async-start(bf16[1,5,1024,256]{3,1,0,2:T(8,128)(2,1)} %copy.18), calls=%async_computation.2 | async-start | bytes 8388608 | tf_op jit(solution)/shard_map/all_to_all | solution.py:39
  208.8 0.2 all-reduce.3.cloned.1.call-start
  209.1 0.0 copy-done.4
  209.1 48.0 %all-to-all-done = bf16[1,5,1024,256]{3,1,0,2:T(8,128)(2,1)} async-done(((bf16[1,5,1024,256]{3,1,0,2:T(8,128)(2,1)}), bf16[1,5,1024,256]{3,1,0,2:T(8,128)(2,1)}, u32[]{:S(2)}, u32[]{:S(2)}) %all-to-all-start) | async-done | bytes 2621472 | tf_op jit(solution)/shard_map/all_to_all | solution.py:39
  257.1 2.8 copy.19
  259.8 0.3 copy.20
  260.1 1.5 copy.21
  261.6 1.7 gather_fusion
  263.3 3.5 fusion.2
  266.8 0.0 copy-start.5
  266.8 1.2 copy.27
  268.0 0.0 all-reduce.3.cloned.1.call-update
  268.0 0.0 reduce-scatter.8.cloned.1.call-start
  268.1 0.0 copy-done.5
  268.1 0.6 dynamic-slice
  269.3 54.8 %all-reduce.3.cloned.1.call-done = f32[40,8192]{1,0:T(8,128)} async-done(((f32[40,8192]{1,0:T(8,128)}), f32[40,8192]{1,0:T(8,128)}) %all-reduce.3.cloned.1.call-update) | async-done | bytes 1310736
  324.1 1.8 constant_dynamic-slice_fusion
  325.9 0.0 reduce-scatter.8.cloned.1.call-update
  325.9 19.5 %reduce-scatter.8.cloned.1.call-done = f32[5,2048]{1,0:T(8,128)} async-done(((f32[5,8192]{1,0:T(8,128)}), f32[5,2048]{1,0:T(8,128)}) %reduce-scatter.8.cloned.1.call-update) | async-done | bytes 40976 | tf_op jit(solution)/shard_map/reduce_scatter | solution.py:55
  (4 shorter events, 0.0 us)
Async XLA Ops:
  6.5 1.0 copy-start
  6.5 64.5 %reduce-scatter.4.cloned.1.call-start = ((), (), s32[]{:S(2)}) async-start(), calls=%async_computation.4 | async-start | bytes 3276800 | tf_op jit(solution)/shard_map/reduce_scatter | solution.py:24
  15.9 0.9 copy-start.2
  15.9 109.3 %reduce-scatter.6.cloned.1.call-start = ((), (), s32[]{:S(2)}) async-start(), calls=%async_computation.6 | async-start | bytes 3276800 | tf_op jit(solution)/shard_map/reduce_scatter | solution.py:23
  25.2 0.7 copy-start.3
  25.2 134.6 %all-gather.3.cloned.1.call-start = ((), (), s32[]{:S(2)}) async-start(), calls=%async_computation.5 | async-start | bytes 1638400 | tf_op jit(solution)/shard_map/all_gather | solution.py:32
  127.6 65.3 %all-gather.5.cloned.1.call-start = ((), (), s32[]{:S(2)}) async-start(), calls=%async_computation.7 | async-start | bytes 1638400 | tf_op jit(solution)/shard_map/all_gather | solution.py:31
  192.9 6.1 %copy-start.1 = (bf16[1,5,1024,128]{2,3,1,0:T(8,128)(2,1)S(1)}, bf16[1,5,1024,128]{2,3,1,0:T(8,128)(2,1)}, u32[]{:S(2)}) copy-start(bf16[1,5,1024,128]{2,3,1,0:T(8,128)(2,1)} %fusion.5) | copy-start | bytes 3932164
  204.1 4.9 %copy-start.4 = (s32[1,1,64]{2,1,0:T(1,128)S(1)}, s32[1,1,64]{2,1,0:T(1,128)}, u32[]{:S(2)}) copy-start(s32[1,1,64]{2,1,0:T(1,128)} %param.12) | copy-start | bytes 772
  204.1 52.9 %all-to-all-start = ((bf16[1,5,1024,256]{3,1,0,2:T(8,128)(2,1)}), bf16[1,5,1024,256]{3,1,0,2:T(8,128)(2,1)}, u32[]{:S(2)}, u32[]{:S(2)}) async-start(bf16[1,5,1024,256]{3,1,0,2:T(8,128)(2,1)} %copy.18), calls=%async_computation.2 | async-start | bytes 8388608 | tf_op jit(solution)/shard_map/all_to_all | solution.py:39
  208.8 115.3 %all-reduce.3.cloned.1.call-start = ((), (), s32[]{:S(2)}) async-start(), calls=%async_computation.9 | async-start | bytes 2621440
  266.8 1.2 copy-start.5
  268.0 77.4 %reduce-scatter.8.cloned.1.call-start = ((), (), s32[]{:S(2)}) async-start(), calls=%async_computation.8 | async-start | bytes 327680 | tf_op jit(solution)/shard_map/reduce_scatter | solution.py:55
Sparse Core Ops, SparseCore 0:
  16.0 54.9 reduce-scatter.3
  73.3 51.7 reduce-scatter.5
  127.7 32.0 all-gather.2
  161.2 31.6 all-gather.4
  268.1 55.9 all-reduce.2
  326.2 19.1 reduce-scatter.7
where the time goes:
time: 353 us; the launch traced here: 352 us
  waiting for transfers between devices  280 us (79%)
  matrix products  33.4 us (9%)
  local copies, waits for them, and re-layouts  17.1 us (5%)
  between operations  14.2 us (4%)
  starting transfers between devices  5.07 us (1%)
    unnamed x7, waiting for transfers between devices  55.4 us
    reduce_scatter x1, waiting for transfers between devices, local(): lax.psum_scatter(reduced_hidden, 'tensor', scatter_dimension=1, tiled=True)  54.1 us
    all_to_all x1, waiting for transfers between devices, local(): lax.all_to_all(direct_gradient, ('dp', 'proj'), split_axis=2, concat_axis...  48 us
    reduce_scatter x1, waiting for transfers between devices, local(): lax.psum_scatter(reduced_upstream, 'tensor', scatter_dimension=1, tiled=T...  45.1 us
    all_gather x1, waiting for transfers between devices, local(): lax.all_gather(upper_share, 'tensor', axis=1, tiled=True)  31.6 us
    all_gather x1, waiting for transfers between devices, local(): lax.all_gather(hidden_share, 'tensor', axis=1, tiled=True)  26 us
    reduce_scatter x1, waiting for transfers between devices, local(): lax.psum_scatter(own_rows, 'tensor', scatter_dimension=1, tiled=True)  19.5 us
    dot_general x1, matrix products, local(): jnp.einsum('spu,un->spn', acts, adapter_down, preferred_element_type=jnp....  8.41 us
  transfers between devices with their start and end apart: 7, of which 7 were waited for; matrix products, arithmetic and copies ran while one was open for 5% of the time, Pallas kernels for 0%

commit v1 on v0

--- a/solution.py
+++ b/solution.py
@@ -36,9 +36,20 @@
     gradient_list = jnp.concatenate([grad_a, grad_b], axis=2).astype(jnp.bfloat16)
     rows_per_range = rows_of_width // (lax.axis_size("dp") * lax.axis_size("proj"))
     direct_gradient = gradient_list.reshape(1, sequence_per_device, rows_of_width, 2 * adapter_rank)
-    landed_blocks = lax.all_to_all(
-        direct_gradient, ("dp", "proj"), split_axis=2, concat_axis=0, tiled=True
-    )
+    ways, here = (lax.axis_size(("dp", "proj")), lax.axis_index(("dp", "proj")))
+    width = direct_gradient.shape[2] // ways
+    shape = list(direct_gradient.shape)
+    shape[2] = width
+    height = shape[0]
+    shape[0] = height * ways
+    landed_blocks = jnp.zeros(shape, direct_gradient.dtype)
+    for mask in range(ways):
+        part = lax.dynamic_slice_in_dim(direct_gradient, (here ^ mask) * width, width, axis=2)
+        if mask:
+            part = lax.ppermute(part, ("dp", "proj"), [(d, d ^ mask) for d in range(ways)])
+        landed_blocks = lax.dynamic_update_slice_in_dim(
+            landed_blocks, part, (here ^ mask) * height, axis=0
+        )
     incoming_blocks = landed_blocks.reshape(-1, rows_per_range, 2 * adapter_rank)
     output_block_count = projection_blocks.shape[2]
     output_block = projection_blocks.shape[4]

time: 353 us -> 339 us (0.960)
  waiting for transfers between devices: 280 us -> 251 us
  local copies, waits for them, and re-layouts: 17.1 us -> 28.2 us
    all_to_all x1 -> x0, waiting for transfers between devices: 48 us -> none  [local(): lax.all_to_all(direct_gradient, ('dp', 'proj'), split_axis=2, concat_axis...]
    ppermute x0 -> x7, waiting for transfers between devices: none -> 16.5 us  [local(): lax.ppermute(part, ('dp', 'proj'), [(d, d ^ mask) for d in range(ways)])]
    another operation x0 -> x8, local copies, waits for them, and re-layouts: none -> 11.6 us
    reduce_scatter x1, waiting for transfers between devices: 54.1 us -> 45 us  [local(): lax.psum_scatter(reduced_hidden, 'tensor', scatter_dimension=1, tiled=True)]
    reduce_scatter x1, waiting for transfers between devices: 45.1 us -> 54.2 us  [local(): lax.psum_scatter(reduced_upstream, 'tensor', scatter_dimension=1, tiled=T...]
    ppermute x0 -> x7, starting transfers between devices: none -> 6.94 us  [local(): lax.ppermute(part, ('dp', 'proj'), [(d, d ^ mask) for d in range(ways)])]
    all_gather x1, waiting for transfers between devices: 26 us -> 31.3 us  [local(): lax.all_gather(hidden_share, 'tensor', axis=1, tiled=True)]
    dynamic_update_slice x0 -> x8, local copies, waits for them, and re-layouts: none -> 5.07 us  [local(): lax.dynamic_update_slice_in_dim(landed_blocks, part, (here ^ mask) * heig...]
  transfers between devices with their start and end apart: 7 -> 13, of which waited for: 7 -> 9; matrix products, arithmetic and copies ran while one was open for 5% -> 9% of each run, Pallas kernels for 0% -> 0%
where the time goes in v1:
time: 339 us; the launch traced here: 338 us
  waiting for transfers between devices  251 us (74%)
  matrix products  31.9 us (9%)
  local copies, waits for them, and re-layouts  28.2 us (8%)
  between operations  14.4 us (4%)
  starting transfers between devices  7.33 us (2%)
  other arithmetic  4.97 us (1%)
    unnamed x7, waiting for transfers between devices  57.7 us
    reduce_scatter x1, waiting for transfers between devices, local(): lax.psum_scatter(reduced_upstream, 'tensor', scatter_dimension=1, tiled=T...  54.2 us
    reduce_scatter x1, waiting for transfers between devices, local(): lax.psum_scatter(reduced_hidden, 'tensor', scatter_dimension=1, tiled=True)  45 us
    all_gather x1, waiting for transfers between devices, local(): lax.all_gather(hidden_share, 'tensor', axis=1, tiled=True)  31.3 us
    all_gather x1, waiting for transfers between devices, local(): lax.all_gather(upper_share, 'tensor', axis=1, tiled=True)  27.1 us
    reduce_scatter x1, waiting for transfers between devices, local(): lax.psum_scatter(own_rows, 'tensor', scatter_dimension=1, tiled=True)  19.5 us
    ppermute x7, waiting for transfers between devices, local(): lax.ppermute(part, ('dp', 'proj'), [(d, d ^ mask) for d in range(ways)])  16.5 us
    another operation x8, local copies, waits for them, and re-layouts  11.6 us
  transfers between devices with their start and end apart: 13, of which 9 were waited for; matrix products, arithmetic and copies ran while one was open for 9% of the time, Pallas kernels for 0%

profile of v1, /device:TPU:0, one launch (start us, length us, event | category | flops | bytes accessed | tf_op | source)
XLA Modules:
  0.0 338.1 jit_solution(624410602041484717)
XLA Ops:
  6.5 0.9 copy-done
  7.5 8.4 %fusion.19 = f32[5,1024,128]{2,1,0:T(8,128)} fusion(bf16[5,1024,1024]{2,1,0:T(8,128)(2,1)} %param.7, bf16[1024,128]{1,0:T(8,128)(2,1)S(1)} %copy-done), kind=kOutput, calls=%fused_computation.40 | convolution fusion | flops 1342177280 | bytes 13369344 | tf_op jit(solution)/shard_map/spu,un->spn/dot_general | solution.py:10
  16.0 0.9 copy-done.2
  16.8 8.4 %fusion.21 = f32[5,1024,128]{2,1,0:T(8,128)} fusion(bf16[5,1024,1024]{2,1,0:T(8,128)(2,1)} %param.8, bf16[128,1024]{1,0:T(8,128)(2,1)S(1)} %copy-done.2), kind=kOutput, calls=%fused_computation.42 | convolution fusion | flops 1342177280 | bytes 13369344 | tf_op jit(solution)/shard_map/iuq,xq->iux/dot_general | solution.py:13
  25.3 0.6 copy-done.3
  25.9 0.1 convert_divide_fusion
  26.0 45.0 %reduce-scatter.6.cloned.1.call-done = f32[5,256,128]{2,1,0:T(8,128)} async-done(((f32[5,1024,128]{2,1,0:T(8,128)}), f32[5,256,128]{2,1,0:T(8,128)}) %reduce-scatter.6.cloned.1.call-update) | async-done | bytes 655376 | tf_op jit(solution)/shard_map/reduce_scatter | solution.py:23
  71.0 54.2 %reduce-scatter.4.cloned.1.call-done = f32[5,256,128]{2,1,0:T(8,128)} async-done(((f32[5,1024,128]{2,1,0:T(8,128)}), f32[5,256,128]{2,1,0:T(8,128)}) %reduce-scatter.4.cloned.1.call-update) | async-done | bytes 655376 | tf_op jit(solution)/shard_map/reduce_scatter | solution.py:24
  125.2 2.4 multiply_convert_fusion
  127.6 0.5 all-gather.3.cloned.1.call-update
  128.2 0.2 all-reduce.3.cloned.1.call-start
  128.5 31.3 %all-gather.5.cloned.1.call-done = bf16[5,1024,128]{2,1,0:T(8,128)(2,1)} async-done(((bf16[5,256,128]{2,1,0:T(8,128)(2,1)}), bf16[5,1024,128]{2,1,0:T(8,128)(2,1)}) %all-gather.5.cloned.1.call-update) | async-done | bytes 1310736 | tf_op jit(solution)/shard_map/all_gather | solution.py:31
  159.8 6.0 %fusion.6 = bf16[5,1024,128]{1,2,0:T(8,128)(2,1)S(1)} fusion(bf16[5,1024,128]{2,1,0:T(8,128)(2,1)} %all-gather.5.cloned.1.call-done, bf16[5,1024,1024]{2,1,0:T(8,128)(2,1)} %param.8), kind=kOutput, calls=%fused_computation.23 | convolution fusion | flops 1342832640 | bytes 13107200 | tf_op jit(solution)/shard_map/etd,etr->edr/dot_general | solution.py:35
  165.8 27.1 %all-gather.3.cloned.1.call-done = bf16[5,1024,128]{2,1,0:T(8,128)(2,1)} async-done(((bf16[5,256,128]{2,1,0:T(8,128)(2,1)}), bf16[5,1024,128]{2,1,0:T(8,128)(2,1)}) %all-gather.3.cloned.1.call-update) | async-done | bytes 1310736 | tf_op jit(solution)/shard_map/all_gather | solution.py:32
  192.9 6.0 %fusion.5 = bf16[5,1024,128]{1,2,0:T(8,128)(2,1)S(1)} fusion(bf16[5,1024,128]{2,1,0:T(8,128)(2,1)} %all-gather.3.cloned.1.call-done, bf16[5,1024,1024]{2,1,0:T(8,128)(2,1)} %param.7), kind=kOutput, calls=%fused_computation.22 | convolution fusion | flops 1342832640 | bytes 13107200 | tf_op jit(solution)/shard_map/etd,etr->edr/dot_general | solution.py:34
  198.9 1.5 fusion.11
  200.4 1.9 copy.24
  202.3 1.5 collective-permute-start
  203.8 1.0 fusion.18
  204.8 1.9 copy.28
  206.7 1.9 copy.23
  208.5 1.9 copy.25
  210.4 1.9 copy.26
  212.3 0.9 copy.27
  213.2 1.5 collective-permute-start.3
  214.7 0.7 collective-permute-start.1
  215.3 1.5 collective-permute-start.4
  216.8 0.3 broadcast_in_dim.19
  217.1 0.2 copy.30
  217.3 1.1 copy.29
  218.5 0.9 collective-permute-start.5
  219.3 1.0 constant_dynamic-update-slice_fusion.6
  220.3 1.0 collective-permute-start.6
  221.3 1.0 constant_dynamic-update-slice_fusion.5
  222.3 8.7 %collective-permute-done.2 = bf16[1,5,128,256]{3,2,1,0:T(8,128)(2,1)} collective-permute-done((bf16[1,5,128,256]{3,2,1,0:T(8,128)(2,1)}, bf16[1,5,128,256]{3,2,1,0:T(8,128)(2,1)}, u32[]{:S(2)}, u32[]{:S(2)}) %collective-permute-start.2) | collective-permute-done | bytes 327712 | tf_op jit(solution)/shard_map/ppermute | solution.py:49
  231.1 1.0 constant_dynamic-update-slice_fusion.4
  232.1 1.0 constant_dynamic-update-slice_fusion.3
  233.1 1.0 constant_dynamic-update-slice_fusion.2
  234.1 3.0 collective-permute-done.5
  237.1 4.9 %collective-permute-done.6 = bf16[1,5,128,256]{3,2,1,0:T(8,128)(2,1)S(1)} collective-permute-done((bf16[1,5,128,256]{3,2,1,0:T(8,128)(2,1)S(1)}, bf16[1,5,128,256]{3,2,1,0:T(8,128)(2,1)S(1)}, u32[]{:S(2)}, u32[]{:S(2)}) %collective-permute-start.6) | collective-permute-done | bytes 327712 | tf_op jit(solution)/shard_map/ppermute | solution.py:49
  242.0 3.0 copy.31
  245.0 2.4 gather_fusion
  247.3 3.1 fusion.2
  250.4 1.1 copy.37
  251.6 0.6 dynamic-slice.32
  252.9 57.1 %all-reduce.3.cloned.1.call-done = f32[40,8192]{1,0:T(8,128)} async-done(((f32[40,8192]{1,0:T(8,128)}), f32[40,8192]{1,0:T(8,128)}) %all-reduce.3.cloned.1.call-update) | async-done | bytes 1310736
  310.0 1.8 constant_dynamic-slice_fusion
  311.7 19.5 %reduce-scatter.8.cloned.1.call-done = f32[5,2048]{1,0:T(8,128)} async-done(((f32[5,8192]{1,0:T(8,128)}), f32[5,2048]{1,0:T(8,128)}) %reduce-scatter.8.cloned.1.call-update) | async-done | bytes 40976 | tf_op jit(solution)/shard_map/reduce_scatter | solution.py:66
  (31 shorter events, 0.4 us)
Async XLA Ops:
  6.5 1.0 copy-start
  6.5 64.5 %reduce-scatter.6.cloned.1.call-start = ((), (), s32[]{:S(2)}) async-start(), calls=%async_computation.5 | async-start | bytes 3276800 | tf_op jit(solution)/shard_map/reduce_scatter | solution.py:23
  15.9 0.9 copy-start.2
  15.9 109.3 %reduce-scatter.4.cloned.1.call-start = ((), (), s32[]{:S(2)}) async-start(), calls=%async_computation.3 | async-start | bytes 3276800 | tf_op jit(solution)/shard_map/reduce_scatter | solution.py:24
  25.2 0.7 copy-start.3
  25.2 103.2 %copy-start.4 = (s32[1,1,64]{2,1,0:T(1,128)S(1)}, s32[1,1,64]{2,1,0:T(1,128)}, u32[]{:S(2)}) copy-start(s32[1,1,64]{2,1,0:T(1,128)} %param.12) | copy-start | bytes 772
  25.3 134.5 %all-gather.5.cloned.1.call-start = ((), (), s32[]{:S(2)}) async-start(), calls=%async_computation.6 | async-start | bytes 1638400 | tf_op jit(solution)/shard_map/all_gather | solution.py:31
  127.6 65.3 %all-gather.3.cloned.1.call-start = ((), (), s32[]{:S(2)}) async-start(), calls=%async_computation.4 | async-start | bytes 1638400 | tf_op jit(solution)/shard_map/all_gather | solution.py:32
  128.2 181.8 %all-reduce.3.cloned.1.call-start = ((), (), s32[]{:S(2)}) async-start(), calls=%async_computation.8 | async-start | bytes 2621440
  202.3 16.2 %collective-permute-start = (bf16[1,5,128,256]{3,2,1,0:T(8,128)(2,1)}, bf16[1,5,128,256]{3,2,1,0:T(8,128)(2,1)}, u32[]{:S(2)}, u32[]{:S(2)}) collective-permute-start(bf16[1,5,128,256]{3,2,1,0:T(8,128)(2,1)} %bitcast.50), channel_id=1, source_target_pairs={{0,1},{1,0},{8,9},{9,8},{16,17},{17,16},{24,25},{25,24},{2,3},{3,2... | collective-permute-start | bytes 983048 | tf_op jit(solution)/shard_map/ppermute | solution.py:49
  213.2 3.9 %copy-start.1 = (bf16[5,128,256]{2,1,0:T(8,128)(2,1)S(1)}, bf16[5,128,256]{2,1,0:T(8,128)(2,1)}, u32[]{:S(2)}) copy-start(bf16[5,128,256]{2,1,0:T(8,128)(2,1)} %copy.23) | copy-start | bytes 983044
  213.2 18.9 %collective-permute-start.3 = (bf16[1,5,128,256]{3,2,1,0:T(8,128)(2,1)}, bf16[1,5,128,256]{3,2,1,0:T(8,128)(2,1)}, u32[]{:S(2)}, u32[]{:S(2)}) collective-permute-start(bf16[1,5,128,256]{3,2,1,0:T(8,128)(2,1)} %bitcast.9), channel_id=1, source_target_pairs={{0,16},{1,17},{8,24},{9,25},{16,0},{17,1},{24,8},{25,9},{2,18},{3,... | collective-permute-start | bytes 983048 | tf_op jit(solution)/shard_map/ppermute | solution.py:49
  214.6 16.4 %collective-permute-start.2 = (bf16[1,5,128,256]{3,2,1,0:T(8,128)(2,1)}, bf16[1,5,128,256]{3,2,1,0:T(8,128)(2,1)}, u32[]{:S(2)}, u32[]{:S(2)}) collective-permute-start(bf16[1,5,128,256]{3,2,1,0:T(8,128)(2,1)} %bitcast.8), channel_id=1, source_target_pairs={{0,9},{1,8},{8,1},{9,0},{16,25},{17,24},{24,17},{25,16},{2,11},{3,... | collective-permute-start | bytes 983048 | tf_op jit(solution)/shard_map/ppermute | solution.py:49
  214.7 5.7 %collective-permute-start.1 = (bf16[1,5,128,256]{3,2,1,0:T(8,128)(2,1)}, bf16[1,5,128,256]{3,2,1,0:T(8,128)(2,1)}, u32[]{:S(2)}, u32[]{:S(2)}) collective-permute-start(bf16[1,5,128,256]{3,2,1,0:T(8,128)(2,1)} %bitcast.7), channel_id=1, source_target_pairs={{0,8},{1,9},{8,0},{9,1},{16,24},{17,25},{24,16},{25,17},{2,10},{3,... | collective-permute-start | bytes 983048 | tf_op jit(solution)/shard_map/ppermute | solution.py:49
  215.3 17.8 %collective-permute-start.4 = (bf16[1,5,128,256]{3,2,1,0:T(8,128)(2,1)}, bf16[1,5,128,256]{3,2,1,0:T(8,128)(2,1)}, u32[]{:S(2)}, u32[]{:S(2)}) collective-permute-start(bf16[1,5,128,256]{3,2,1,0:T(8,128)(2,1)} %bitcast.10), channel_id=1, source_target_pairs={{0,17},{1,16},{8,25},{9,24},{16,1},{17,0},{24,9},{25,8},{2,19},{3,... | collective-permute-start | bytes 983048 | tf_op jit(solution)/shard_map/ppermute | solution.py:49
  218.5 18.6 %collective-permute-start.5 = (bf16[1,5,128,256]{3,2,1,0:T(8,128)(2,1)S(1)}, bf16[1,5,128,256]{3,2,1,0:T(8,128)(2,1)S(1)}, u32[]{:S(2)}, u32[]{:S(2)}) collective-permute-start(bf16[1,5,128,256]{3,2,1,0:T(8,128)(2,1)S(1)} %bitcast.51), channel_id=1, source_target_pairs={{0,24},{1,25},{8,16},{9,17},{16,8},{17,9},{24,0},{25,1},{2,26},{3,... | collective-permute-start | bytes 983048 | tf_op jit(solution)/shard_map/ppermute | solution.py:49
  220.3 21.6 %collective-permute-start.6 = (bf16[1,5,128,256]{3,2,1,0:T(8,128)(2,1)S(1)}, bf16[1,5,128,256]{3,2,1,0:T(8,128)(2,1)S(1)}, u32[]{:S(2)}, u32[]{:S(2)}) collective-permute-start(bf16[1,5,128,256]{3,2,1,0:T(8,128)(2,1)S(1)} %bitcast.49), channel_id=1, source_target_pairs={{0,25},{1,24},{8,17},{9,16},{16,9},{17,8},{24,1},{25,0},{2,27},{3,... | collective-permute-start | bytes 983048 | tf_op jit(solution)/shard_map/ppermute | solution.py:49
  250.4 1.2 copy-start.5
  251.6 79.6 %reduce-scatter.8.cloned.1.call-start = ((), (), s32[]{:S(2)}) async-start(), calls=%async_computation.7 | async-start | bytes 327680 | tf_op jit(solution)/shard_map/reduce_scatter | solution.py:66
Sparse Core Ops, SparseCore 0:
  16.0 54.9 reduce-scatter.5
  73.3 51.8 reduce-scatter.3
  127.7 32.0 all-gather.4
  161.2 31.6 all-gather.2
  251.7 58.2 all-reduce.2
  312.1 19.1 reduce-scatter.7
